TPU v7x, 128 devices: a whole 4x4x4 slice. The times are simulated.
128 devices in a mesh: segment: 8 (over z_hi, y), patch: 16 (over x, z_lo, core).
Axes of the slice: x: 4, y: 4, z: 4 (z_hi: 2, z_lo: 2; z = z_hi * 2 + z_lo), core: 2. Of those that a mesh axis runs over, the one named last changes fastest.
Arguments:
- features: bfloat16 [8, 2, 320, 64, 128], P('segment', None, None, 'patch'), may hold values from -48 to 48, as said below
- latent: float32 [2, 4, 64, 128], P(None, None, 'patch'), may hold values from -48 to 48
- plan_pos: int32 [2], replicated, may hold values from 0 to 9
- blocks_used: int32 [8], P('segment'), may hold values from 1 to 2, as said below
- conv1_w: bfloat16 [8, 2, 9, 320, 320], P('segment'), may hold values from -0.109375 to 0.109375
- conv2_w: bfloat16 [8, 2, 9, 320, 320], P('segment'), may hold values from -0.109375 to 0.109375
- norm_gain: float32 [8, 2, 2, 320], P('segment'), may hold values from 0.25 to 1.75
- norm_shift: float32 [8, 2, 2, 320], P('segment'), may hold values from -3 to 3
- in_w: bfloat16 [9, 320, 4], replicated, may hold values from -1 to 1
- head_w: bfloat16 [9, 4, 320], replicated, may hold values from -0.109375 to 0.109375
- head_gain: float32 [320], replicated, may hold values from 0.25 to 1.75
- head_shift: float32 [320], replicated, may hold values from -3 to 3
Outputs:
- latent_out: float32 [2, 4, 64, 128], P(None, None, 'patch', 'segment')
- features_out: bfloat16 [8, 2, 320, 64, 128], P('segment', None, None, 'patch')
Inputs may be any that keep to these rules, and one draw needn't show every extreme that they name: `features`: every entry lies within the range; row magnitudes vary over the rows. `blocks_used`: each section holds 1 or 2 blocks; both counts occur.
All inputs are finite; a program needn't handle non-finite values.
Results may differ from a plain program's by a relative error of at most 0.0075.
Values may be sent and summed in bfloat16 or wider, within the bound.
A program may use at most 64 MiB of HBM per device.

v0:
```python
import jax
import jax.numpy as jnp
from jax import lax
from jax.sharding import PartitionSpec as P

GROUPS = 32
STEPS = 2
SCHED = 12
epsilon = 1e-05
sigma_top = 3.0
sigma_low = 0.1
rho_power = 7.0


def with_halo(block, sides, width):
    for axis, dim in sides:
        count = lax.axis_size(axis)
        forward = [(i, i + 1) for i in range(count - 1)]
        backward = [(target, source) for source, target in forward]
        low = lax.ppermute(
            lax.slice_in_dim(block, block.shape[dim] - width, None, axis=dim), axis, forward
        )
        high = lax.ppermute(lax.slice_in_dim(block, 0, width, axis=dim), axis, backward)
        block = jnp.concatenate([low, block, high], axis=dim)
    return block


def from_behind(shard, axis, by):
    devices = lax.axis_size(axis)
    pairs = [(i, i + by) for i in range(devices) if 0 <= i + by < devices]
    return lax.ppermute(shard, axis, pairs)


def broadcast(shard, axis, root):
    mine = lax.axis_index(axis) == root
    return lax.psum(jnp.where(mine, shard, jnp.zeros_like(shard)), axis)


def sigma_at(position):
    fraction = position.astype(jnp.float32) / (SCHED - 1)
    top_root = sigma_top ** (1.0 / rho_power)
    low_root = sigma_low ** (1.0 / rho_power)
    return (top_root + fraction * (low_root - top_root)) ** rho_power


def group_moments(values):
    batch_size, chan_count, height, col_count = values.shape
    grouped = values.reshape(batch_size, GROUPS, chan_count // GROUPS, height, col_count)
    cell_count = chan_count // GROUPS * height * col_count * lax.axis_size("patch")
    center = lax.psum(jnp.sum(grouped, axis=(2, 3, 4)), "patch") / cell_count
    deviation = grouped - center[:, :, None, None, None]
    spread = lax.psum(jnp.sum(jnp.square(deviation), axis=(2, 3, 4)), "patch") / cell_count
    return (center, jnp.sqrt(spread + epsilon))


def norm_silu(values, moments, gain, shift):
    center, root_spread = moments
    batch_size, chan_count, height, col_count = values.shape
    grouped = values.reshape(batch_size, GROUPS, chan_count // GROUPS, height, col_count)
    normed = (
        (grouped - center[:, :, None, None, None]) / root_spread[:, :, None, None, None]
    ).reshape(values.shape)
    normed = normed * gain[None, :, None, None] + shift[None, :, None, None]
    return jax.nn.silu(normed)


def conv_valid(rows_in, kernel):
    padded = jnp.pad(rows_in, ((0, 0), (0, 0), (0, 0), (1, 1)))
    height = rows_in.shape[2] - 2
    col_count = rows_in.shape[3]
    accum = jnp.zeros((rows_in.shape[0], kernel.shape[1], height, col_count), jnp.float32)
    for tap_no in range(9):
        row_off, col_off = (tap_no // 3, tap_no % 3)
        window = padded[:, :, row_off : row_off + height, col_off : col_off + col_count]
        accum = accum + jnp.einsum(
            "oi,bihw->bohw", kernel[tap_no], window, preferred_element_type=jnp.float32
        )
    return accum


def with_rows(values):
    return with_halo(values, (("patch", 2),), 1)


def resnet_unit(hidden, kern_one, kern_two, gain_pair, shift_pair):
    hidden_wide = hidden.astype(jnp.float32)
    first_act = norm_silu(
        hidden_wide, group_moments(hidden_wide), gain_pair[0], shift_pair[0]
    ).astype(jnp.bfloat16)
    middle = conv_valid(with_rows(first_act), kern_one)
    second = norm_silu(middle, group_moments(middle), gain_pair[1], shift_pair[1]).astype(
        jnp.bfloat16
    )
    result = conv_valid(with_rows(second), kern_two)
    return (hidden_wide + result).astype(jnp.bfloat16)


def head_noise(source, head_w, head_gain, head_shift):
    source_wide = source.astype(jnp.float32)
    head_input = norm_silu(source_wide, group_moments(source_wide), head_gain, head_shift).astype(
        jnp.bfloat16
    )
    return conv_valid(with_rows(head_input), head_w)


def per_device(
    features,
    latent,
    plan_pos,
    blocks_used,
    conv1_w,
    conv2_w,
    norm_gain,
    norm_shift,
    in_w,
    head_w,
    head_gain,
    head_shift,
):
    segment_count = lax.axis_size("segment")
    segment_pos = lax.axis_index("segment")
    current = features[0]
    for step_no in range(STEPS):
        arrived = from_behind(current, "segment", 1)
        noise_local = head_noise(current, head_w, head_gain, head_shift)
        noise_pred = broadcast(noise_local, "segment", segment_count - 1)
        position = plan_pos + step_no
        sigma_now = sigma_at(position)
        sigma_next = sigma_at(position + 1)
        latent = latent + (sigma_next - sigma_now)[:, None, None, None] * noise_pred
        scaled = (latent / jnp.sqrt(sigma_next * sigma_next + 1.0)[:, None, None, None]).astype(
            jnp.bfloat16
        )
        entry_rows = conv_valid(with_rows(scaled), in_w).astype(jnp.bfloat16)
        source = jnp.where(segment_pos == 0, entry_rows, arrived)
        after_one = resnet_unit(
            source, conv1_w[0, 0], conv2_w[0, 0], norm_gain[0, 0], norm_shift[0, 0]
        )
        after_two = resnet_unit(
            after_one, conv1_w[0, 1], conv2_w[0, 1], norm_gain[0, 1], norm_shift[0, 1]
        )
        current = jnp.where(blocks_used[0] >= 2, after_two, after_one)
    col_share = latent.shape[3] // segment_count
    latent_part = lax.dynamic_slice_in_dim(latent, segment_pos * col_share, col_share, 3)
    return (latent_part, current[None])


def solution(mesh):
    placed = (
        P("segment", None, None, "patch", None),
        P(None, None, "patch", None),
        P(),
        P("segment"),
        P("segment", None, None, None, None),
        P("segment", None, None, None, None),
        P("segment", None, None, None),
        P("segment", None, None, None),
        P(),
        P(),
        P(),
        P(),
    )
    return jax.shard_map(
        per_device,
        mesh=mesh,
        in_specs=placed,
        out_specs=(P(None, None, "patch", "segment"), P("segment", None, None, "patch", None)),
        check_vma=False,
    )
```

profile of v0, /device:TPU:65, one launch (start us, length us, event | category | flops | bytes accessed | tf_op | source)
XLA Modules:
  0.0 886.7 jit_solution(16695528666948445930)
XLA Ops:
  3.2 27.2 %psum.154 = f32[2,32]{1,0:T(2,128)S(1)} all-reduce(f32[2,32]{1,0:T(2,128)S(1)} %reduce_sum.235), channel_id=1, replica_groups=mesh['segment'=8,'patch'=16] {'patch'}, use_global_device_ids=true, to_apply=%region_2.0 | all-reduce | flops 64 | bytes 512 | tf_op jit(solution)/shard_map/psum | solution.py:50
  30.7 8.3 fusion.81
  39.2 30.3 %psum.155 = f32[2,32]{1,0:T(2,128)S(1)} all-reduce(f32[2,32]{1,0:T(2,128)S(1)} %reduce_sum.241), channel_id=1, replica_groups=mesh['segment'=8,'patch'=16] {'patch'}, use_global_device_ids=true, to_apply=%region_5.6 | all-reduce | flops 64 | bytes 512 | tf_op jit(solution)/shard_map/psum | solution.py:52
  73.1 3.2 collective-permute-start.1
  76.3 3.2 collective-permute-start.4
  87.4 33.3 %psum.156 = f32[2,4,4,128]{3,1,2,0:T(4,128)S(1)} all-reduce(f32[2,4,4,128]{3,1,2,0:T(4,128)S(1)} %fusion.115), channel_id=1, replica_groups=mesh['segment'=8,'patch'=16] {'segment'}, use_global_device_ids=true, to_apply=%region_6.7 | all-reduce | flops 4096 | bytes 32768 | tf_op jit(solution)/shard_map/psum | solution.py:36
  120.8 9.9 %collective-permute-start.2 = (bf16[2,4,1,128]{3,1,2,0:T(4,128)(2,1)S(1)}, bf16[2,4,1,128]{3,1,2,0:T(4,128)(2,1)S(1)}, u32[]{:S(2)}, u32[]{:S(2)}) collective-permute-start(bf16[2,4,1,128]{3,1,2,0:T(4,128)(2,1)S(1)} %get-tuple-element.38), channel_id=1, source_target_pairs={{0,1},{1,2},{2,3},{3,4},{4,5},{5,6},{6,7},{7,8},{8,9},{9,10},{10,1... | collective-permute-start | bytes 6152 | tf_op jit(solution)/shard_map/ppermute | solution.py:20
  140.0 24.6 %psum.157 = f32[2,32]{1,0:T(2,128)S(1)} all-reduce(f32[2,32]{1,0:T(2,128)S(1)} %reduce_sum.247), channel_id=1, replica_groups=mesh['segment'=8,'patch'=16] {'patch'}, use_global_device_ids=true, to_apply=%region_9.10 | all-reduce | flops 64 | bytes 512 | tf_op jit(solution)/shard_map/psum | solution.py:50
  165.4 29.9 %psum.158 = f32[2,32]{1,0:T(2,128)S(1)} all-reduce(f32[2,32]{1,0:T(2,128)S(1)} %reduce_sum.250), channel_id=1, replica_groups=mesh['segment'=8,'patch'=16] {'patch'}, use_global_device_ids=true, to_apply=%region_12.13 | all-reduce | flops 64 | bytes 512 | tf_op jit(solution)/shard_map/psum | solution.py:52
  202.1 2.6 collective-permute-done.6
  218.2 23.6 %psum.159 = f32[2,32]{1,0:T(2,128)S(1)} all-reduce(f32[2,32]{1,0:T(2,128)S(1)} %reduce_sum.256), channel_id=1, replica_groups=mesh['segment'=8,'patch'=16] {'patch'}, use_global_device_ids=true, to_apply=%region_15.16 | all-reduce | flops 64 | bytes 512 | tf_op jit(solution)/shard_map/psum | solution.py:50
  242.5 30.5 %psum.160 = f32[2,32]{1,0:T(2,128)S(1)} all-reduce(f32[2,32]{1,0:T(2,128)S(1)} %reduce_sum.262), channel_id=1, replica_groups=mesh['segment'=8,'patch'=16] {'patch'}, use_global_device_ids=true, to_apply=%region_18.19 | all-reduce | flops 64 | bytes 512 | tf_op jit(solution)/shard_map/psum | solution.py:52
  279.8 2.6 collective-permute-done.8
  296.0 23.8 %psum.161 = f32[2,32]{1,0:T(2,128)S(1)} all-reduce(f32[2,32]{1,0:T(2,128)S(1)} %reduce_sum.265), channel_id=1, replica_groups=mesh['segment'=8,'patch'=16] {'patch'}, use_global_device_ids=true, to_apply=%region_21.22 | all-reduce | flops 64 | bytes 512 | tf_op jit(solution)/shard_map/psum | solution.py:50
  320.6 30.5 %psum.162 = f32[2,32]{1,0:T(2,128)S(1)} all-reduce(f32[2,32]{1,0:T(2,128)S(1)} %reduce_sum.271), channel_id=1, replica_groups=mesh['segment'=8,'patch'=16] {'patch'}, use_global_device_ids=true, to_apply=%region_24.25 | all-reduce | flops 64 | bytes 512 | tf_op jit(solution)/shard_map/psum | solution.py:52
  357.9 2.6 collective-permute-done.10
  374.0 23.6 %psum.163 = f32[2,32]{1,0:T(2,128)S(1)} all-reduce(f32[2,32]{1,0:T(2,128)S(1)} %reduce_sum.277), channel_id=1, replica_groups=mesh['segment'=8,'patch'=16] {'patch'}, use_global_device_ids=true, to_apply=%region_27.28 | all-reduce | flops 64 | bytes 512 | tf_op jit(solution)/shard_map/psum | solution.py:50
  398.3 30.5 %psum.164 = f32[2,32]{1,0:T(2,128)S(1)} all-reduce(f32[2,32]{1,0:T(2,128)S(1)} %reduce_sum.280), channel_id=1, replica_groups=mesh['segment'=8,'patch'=16] {'patch'}, use_global_device_ids=true, to_apply=%region_30.31 | all-reduce | flops 64 | bytes 512 | tf_op jit(solution)/shard_map/psum | solution.py:52
  451.9 23.6 %psum.165 = f32[2,32]{1,0:T(2,128)S(1)} all-reduce(f32[2,32]{1,0:T(2,128)S(1)} %reduce_sum.286), channel_id=1, replica_groups=mesh['segment'=8,'patch'=16] {'patch'}, use_global_device_ids=true, to_apply=%region_33.34 | all-reduce | flops 64 | bytes 512 | tf_op jit(solution)/shard_map/psum | solution.py:50
  478.2 30.8 %psum.166 = f32[2,32]{1,0:T(2,128)S(1)} all-reduce(f32[2,32]{1,0:T(2,128)S(1)} %reduce_sum.292), channel_id=1, replica_groups=mesh['segment'=8,'patch'=16] {'patch'}, use_global_device_ids=true, to_apply=%region_36.37 | all-reduce | flops 64 | bytes 512 | tf_op jit(solution)/shard_map/psum | solution.py:52
  515.7 2.6 collective-permute-done.14
  521.5 34.6 %psum.167 = f32[2,4,4,128]{3,1,2,0:T(4,128)S(1)} all-reduce(f32[2,4,4,128]{3,1,2,0:T(4,128)S(1)} %fusion.107), channel_id=1, replica_groups=mesh['segment'=8,'patch'=16] {'segment'}, use_global_device_ids=true, to_apply=%region_37.38 | all-reduce | flops 4096 | bytes 32768 | tf_op jit(solution)/shard_map/psum | solution.py:36
  556.2 9.6 %collective-permute-start.15 = (bf16[2,4,1,128]{3,1,2,0:T(4,128)(2,1)S(1)}, bf16[2,4,1,128]{3,1,2,0:T(4,128)(2,1)S(1)}, u32[]{:S(2)}, u32[]{:S(2)}) collective-permute-start(bf16[2,4,1,128]{3,1,2,0:T(4,128)(2,1)S(1)} %get-tuple-element.36), channel_id=1, source_target_pairs={{0,1},{1,2},{2,3},{3,4},{4,5},{5,6},{6,7},{7,8},{8,9},{9,10},{10,1... | collective-permute-start | bytes 6152 | tf_op jit(solution)/shard_map/ppermute | solution.py:20
  574.3 24.6 %psum.168 = f32[2,32]{1,0:T(2,128)S(1)} all-reduce(f32[2,32]{1,0:T(2,128)S(1)} %reduce_sum.295), channel_id=1, replica_groups=mesh['segment'=8,'patch'=16] {'patch'}, use_global_device_ids=true, to_apply=%region_40.41 | all-reduce | flops 64 | bytes 512 | tf_op jit(solution)/shard_map/psum | solution.py:50
  599.7 29.5 %psum.169 = f32[2,32]{1,0:T(2,128)S(1)} all-reduce(f32[2,32]{1,0:T(2,128)S(1)} %reduce_sum.361), channel_id=1, replica_groups=mesh['segment'=8,'patch'=16] {'patch'}, use_global_device_ids=true, to_apply=%region_43.44 | all-reduce | flops 64 | bytes 512 | tf_op jit(solution)/shard_map/psum | solution.py:52
  635.9 2.6 collective-permute-done.19
  651.9 23.6 %psum.170 = f32[2,32]{1,0:T(2,128)S(1)} all-reduce(f32[2,32]{1,0:T(2,128)S(1)} %reduce_sum.364), channel_id=1, replica_groups=mesh['segment'=8,'patch'=16] {'patch'}, use_global_device_ids=true, to_apply=%region_46.47 | all-reduce | flops 64 | bytes 512 | tf_op jit(solution)/shard_map/psum | solution.py:50
  676.3 30.5 %psum.171 = f32[2,32]{1,0:T(2,128)S(1)} all-reduce(f32[2,32]{1,0:T(2,128)S(1)} %reduce_sum.367), channel_id=1, replica_groups=mesh['segment'=8,'patch'=16] {'patch'}, use_global_device_ids=true, to_apply=%region_49.50 | all-reduce | flops 64 | bytes 512 | tf_op jit(solution)/shard_map/psum | solution.py:52
  729.7 23.6 %psum.172 = f32[2,32]{1,0:T(2,128)S(1)} all-reduce(f32[2,32]{1,0:T(2,128)S(1)} %reduce_sum.370), channel_id=1, replica_groups=mesh['segment'=8,'patch'=16] {'patch'}, use_global_device_ids=true, to_apply=%region_52.53 | all-reduce | flops 64 | bytes 512 | tf_op jit(solution)/shard_map/psum | solution.py:50
  754.1 30.5 %psum.173 = f32[2,32]{1,0:T(2,128)S(1)} all-reduce(f32[2,32]{1,0:T(2,128)S(1)} %reduce_sum.373), channel_id=1, replica_groups=mesh['segment'=8,'patch'=16] {'patch'}, use_global_device_ids=true, to_apply=%region_55.56 | all-reduce | flops 64 | bytes 512 | tf_op jit(solution)/shard_map/psum | solution.py:52
  807.4 23.6 %psum.174 = f32[2,32]{1,0:T(2,128)S(1)} all-reduce(f32[2,32]{1,0:T(2,128)S(1)} %reduce_sum.376), channel_id=1, replica_groups=mesh['segment'=8,'patch'=16] {'patch'}, use_global_device_ids=true, to_apply=%region_58.59 | all-reduce | flops 64 | bytes 512 | tf_op jit(solution)/shard_map/psum | solution.py:50
  831.8 30.7 %psum.175 = f32[2,32]{1,0:T(2,128)S(1)} all-reduce(f32[2,32]{1,0:T(2,128)S(1)} %reduce_sum.379), channel_id=1, replica_groups=mesh['segment'=8,'patch'=16] {'patch'}, use_global_device_ids=true, to_apply=%region_61.62 | all-reduce | flops 64 | bytes 512 | tf_op jit(solution)/shard_map/psum | solution.py:52
  (322 shorter events, 222.5 us)
Async XLA Ops:
  0.6 69.1 %copy-start = (bf16[1,2,320,4,128]{4,3,2,1,0:T(4,128)(2,1)S(1)}, bf16[1,2,320,4,128]{4,3,2,1,0:T(4,128)(2,1)}, u32[]{:S(2)}) copy-start(bf16[1,2,320,4,128]{4,3,2,1,0:T(4,128)(2,1)} %param.12) | copy-start | bytes 1966084
  0.6 69.1 %copy-start.4 = (f32[320]{0:T(512)S(1)}, f32[320]{0:T(512)}, u32[]{:S(2)}) copy-start(f32[320]{0:T(512)} %param.22) | copy-start | bytes 3844
  0.7 69.1 %copy-start.3 = (f32[320]{0:T(512)S(1)}, f32[320]{0:T(512)}, u32[]{:S(2)}) copy-start(f32[320]{0:T(512)} %param.23) | copy-start | bytes 3844
  71.1 11.3 %collective-permute-start = (bf16[2,320,1,128]{3,1,2,0:T(8,128)(2,1)}, bf16[2,320,1,128]{3,1,2,0:T(8,128)(2,1)}, u32[]{:S(2)}, u32[]{:S(2)}) collective-permute-start(bf16[2,320,1,128]{3,1,2,0:T(8,128)(2,1)} %get-tuple-element.34), channel_id=1, source_target_pairs={{0,1},{1,2},{2,3},{3,4},{4,5},{5,6},{6,7},{7,8},{8,9},{9,10},{10,1... | collective-permute-start | bytes 491528 | tf_op jit(solution)/shard_map/ppermute | solution.py:20
  73.1 9.3 %collective-permute-start.1 = (bf16[2,320,1,128]{3,1,2,0:T(8,128)(2,1)}, bf16[2,320,1,128]{3,1,2,0:T(8,128)(2,1)S(1)}, u32[]{:S(2)}, u32[]{:S(2)}) collective-permute-start(bf16[2,320,1,128]{3,1,2,0:T(8,128)(2,1)} %get-tuple-element.35), channel_id=1, source_target_pairs={{1,0},{2,1},{3,2},{4,3},{5,4},{6,5},{7,6},{8,7},{9,8},{10,9},{11,1... | collective-permute-start | bytes 491528 | tf_op jit(solution)/shard_map/ppermute | solution.py:23
  76.3 62.8 %collective-permute-start.4 = (bf16[2,320,4,128]{3,1,2,0:T(8,128)(2,1)S(1)}, bf16[2,320,4,128]{3,1,2,0:T(8,128)(2,1)S(1)}, u32[]{:S(2)}, u32[]{:S(2)}) collective-permute-start(bf16[2,320,4,128]{3,1,2,0:T(8,128)(2,1)S(1)} %bitcast.575), channel_id=1, source_target_pairs={{0,16},{16,32},{32,48},{48,64},{64,80},{80,96},{96,112},{1,17},{17... | collective-permute-start | bytes 1966088 | tf_op jit(solution)/shard_map/ppermute | solution.py:31
  86.8 44.0 %copy-start.5 = (f32[1,2,2,320]{3,2,1,0:T(2,128)S(1)}, f32[1,2,2,320]{3,2,1,0:T(2,128)}, u32[]{:S(2)}) copy-start(f32[1,2,2,320]{3,2,1,0:T(2,128)} %param.19) | copy-start | bytes 15364
  86.8 44.0 %copy-start.6 = (f32[1,2,2,320]{3,2,1,0:T(2,128)S(1)}, f32[1,2,2,320]{3,2,1,0:T(2,128)}, u32[]{:S(2)}) copy-start(f32[1,2,2,320]{3,2,1,0:T(2,128)} %param.18) | copy-start | bytes 15364
  86.8 46.6 %copy-start.1 = (bf16[9,320,4]{1,2,0:T(4,128)(2,1)S(1)}, bf16[9,320,4]{1,2,0:T(4,128)(2,1)}, u32[]{:S(2)}) copy-start(bf16[9,320,4]{1,2,0:T(4,128)(2,1)} %param.20) | copy-start | bytes 69124
  120.8 12.6 %collective-permute-start.2 = (bf16[2,4,1,128]{3,1,2,0:T(4,128)(2,1)S(1)}, bf16[2,4,1,128]{3,1,2,0:T(4,128)(2,1)S(1)}, u32[]{:S(2)}, u32[]{:S(2)}) collective-permute-start(bf16[2,4,1,128]{3,1,2,0:T(4,128)(2,1)S(1)} %get-tuple-element.38), channel_id=1, source_target_pairs={{0,1},{1,2},{2,3},{3,4},{4,5},{5,6},{6,7},{7,8},{8,9},{9,10},{10,1... | collective-permute-start | bytes 6152 | tf_op jit(solution)/shard_map/ppermute | solution.py:20
  131.5 4.9 collective-permute-start.3
  196.2 5.9 collective-permute-start.5
  198.1 6.6 collective-permute-start.6
  273.9 5.9 collective-permute-start.7
  275.8 6.6 collective-permute-start.8
  352.0 5.9 collective-permute-start.9
  353.9 6.6 collective-permute-start.10
  429.7 6.0 collective-permute-start.11
  431.6 6.6 collective-permute-start.12
  475.7 97.7 %collective-permute-start.17 = (bf16[2,320,4,128]{3,1,2,0:T(8,128)(2,1)S(1)}, bf16[2,320,4,128]{3,1,2,0:T(8,128)(2,1)S(1)}, u32[]{:S(2)}, u32[]{:S(2)}) collective-permute-start(bf16[2,320,4,128]{3,1,2,0:T(8,128)(2,1)S(1)} %get-tuple-element.53), channel_id=1, source_target_pairs={{0,16},{16,32},{32,48},{48,64},{64,80},{80,96},{96,112},{1,17},{17... | collective-permute-start | bytes 1966088 | tf_op jit(solution)/shard_map/ppermute | solution.py:31
  509.8 5.9 collective-permute-start.13
  511.7 6.6 collective-permute-start.14
  556.2 12.6 %collective-permute-start.15 = (bf16[2,4,1,128]{3,1,2,0:T(4,128)(2,1)S(1)}, bf16[2,4,1,128]{3,1,2,0:T(4,128)(2,1)S(1)}, u32[]{:S(2)}, u32[]{:S(2)}) collective-permute-start(bf16[2,4,1,128]{3,1,2,0:T(4,128)(2,1)S(1)} %get-tuple-element.36), channel_id=1, source_target_pairs={{0,1},{1,2},{2,3},{3,4},{4,5},{5,6},{6,7},{7,8},{8,9},{9,10},{10,1... | collective-permute-start | bytes 6152 | tf_op jit(solution)/shard_map/ppermute | solution.py:20
  565.8 4.9 collective-permute-start.16
  630.0 5.9 collective-permute-start.18
  631.9 6.6 collective-permute-start.19
  707.6 6.0 collective-permute-start.20
  709.6 6.6 collective-permute-start.21
  785.5 5.9 collective-permute-start.22
  787.4 6.6 collective-permute-start.23
  863.3 5.9 collective-permute-start.24
  865.3 6.6 collective-permute-start.25
  (3 other events, 49.1 us)
where the time goes:
time: 898 us; the launch traced here: 887 us
  blocking collectives  614 us (68%)
  matrix products  122 us (14%)
  starting transfers between devices  73.3 us (8%)
  other arithmetic  35.6 us (4%)
  waiting for transfers between devices  29.8 us (3%)
  local copies, waits for them, and re-layouts  9.08 us (1%)
    psum x10, blocking collectives, group_moments(): lax.psum(jnp.sum(jnp.square(deviation), axis=(2, 3, 4)), 'patch')  304 us
    psum x10, blocking collectives, group_moments(): center = lax.psum(jnp.sum(grouped, axis=(2, 3, 4)), 'patch') / cell_count  242 us
    dot_general x108, matrix products, conv_valid(): jnp.einsum('oi,bihw->bohw', kernel[tap_no], window, preferred_element_typ...  122 us
    psum x2, blocking collectives, broadcast(): return lax.psum(jnp.where(mine, shard, jnp.zeros_like(shard)), axis)  67.9 us
    ppermute x12, starting transfers between devices, with_halo(): lax.ppermute(lax.slice_in_dim(block, block.shape[dim] - width, None, axis...  38.7 us
    ppermute x12, starting transfers between devices, with_halo(): lax.ppermute(lax.slice_in_dim(block, 0, width, axis=dim), axis, backward)  29.5 us
    ppermute x12, waiting for transfers between devices, with_halo(): lax.ppermute(lax.slice_in_dim(block, 0, width, axis=dim), axis, backward)  27.7 us
  transfers between devices with their start and end apart: 26, of which 18 were waited for; matrix products, arithmetic and copies ran while one was open for 4% of the time, Pallas kernels for 0%

commit v1 on v0

--- a/solution.py
+++ b/solution.py
@@ -1,3 +1,4 @@
+import functools
 import jax
 import jax.numpy as jnp
 from jax import lax
@@ -10,6 +11,15 @@
 sigma_top = 3.0
 sigma_low = 0.1
 rho_power = 7.0
+
+
+def mix_arrays(work_x, along_axis):
+    parts_out = jax.lax.all_gather(work_x, along_axis)
+    all_values = jnp.sum(parts_out, 0)
+    return all_values
+
+
+roads_trace = functools.partial(mix_arrays, along_axis="patch")
 
 
 def with_halo(block, sides, width):
@@ -47,7 +57,7 @@
     batch_size, chan_count, height, col_count = values.shape
     grouped = values.reshape(batch_size, GROUPS, chan_count // GROUPS, height, col_count)
     cell_count = chan_count // GROUPS * height * col_count * lax.axis_size("patch")
-    center = lax.psum(jnp.sum(grouped, axis=(2, 3, 4)), "patch") / cell_count
+    center = roads_trace(jnp.sum(grouped, axis=(2, 3, 4))) / cell_count
     deviation = grouped - center[:, :, None, None, None]
     spread = lax.psum(jnp.sum(jnp.square(deviation), axis=(2, 3, 4)), "patch") / cell_count
     return (center, jnp.sqrt(spread + epsilon))

time: 898 us -> 788 us (0.88)
  blocking collectives: 614 us -> 503 us
    psum x10 -> x0, blocking collectives: 242 us -> none  [group_moments(): center = lax.psum(jnp.sum(grouped, axis=(2, 3, 4)), 'patch') / cell_count]
    all_gather x0 -> x10, blocking collectives: none -> 167 us  [mix_arrays(): parts_out = jax.lax.all_gather(work_x, along_axis)]
    psum x10, blocking collectives: 304 us -> 268 us  [group_moments(): lax.psum(jnp.sum(jnp.square(deviation), axis=(2, 3, 4)), 'patch')]
where the time goes in v1:
time: 788 us; the launch traced here: 776 us
  blocking collectives  503 us (64%)
  matrix products  122 us (15%)
  starting transfers between devices  73.2 us (9%)
  other arithmetic  35.9 us (5%)
  waiting for transfers between devices  29.9 us (4%)
  local copies, waits for them, and re-layouts  9.08 us (1%)
    psum x10, blocking collectives, group_moments(): lax.psum(jnp.sum(jnp.square(deviation), axis=(2, 3, 4)), 'patch')  268 us
    all_gather x10, blocking collectives, mix_arrays(): parts_out = jax.lax.all_gather(work_x, along_axis)  167 us
    dot_general x108, matrix products, conv_valid(): jnp.einsum('oi,bihw->bohw', kernel[tap_no], window, preferred_element_typ...  122 us
    psum x2, blocking collectives, broadcast(): return lax.psum(jnp.where(mine, shard, jnp.zeros_like(shard)), axis)  67.7 us
    ppermute x12, starting transfers between devices, with_halo(): lax.ppermute(lax.slice_in_dim(block, block.shape[dim] - width, None, axis...  38.6 us
    ppermute x12, starting transfers between devices, with_halo(): lax.ppermute(lax.slice_in_dim(block, 0, width, axis=dim), axis, backward)  29.5 us
    ppermute x12, waiting for transfers between devices, with_halo(): lax.ppermute(lax.slice_in_dim(block, 0, width, axis=dim), axis, backward)  27.7 us
  transfers between devices with their start and end apart: 26, of which 18 were waited for; matrix products, arithmetic and copies ran while one was open for 4% of the time, Pallas kernels for 0%

profile of v1, /device:TPU:65, one launch (start us, length us, event | category | flops | bytes accessed | tf_op | source)
XLA Modules:
  0.0 776.0 jit_solution(15318753480237743719)
XLA Ops:
  3.2 20.2 %all-gather.10 = f32[16,2,32]{2,1,0:T(2,128)S(1)} all-gather(f32[1,2,32]{2,1,0:T(2,128)S(1)} %bitcast.586), channel_id=2, replica_groups=mesh['segment'=8,'patch'=16] {'patch'}, dimensions={0}, use_global_device_ids=true | all-gather | bytes 4352 | tf_op jit(solution)/shard_map/all_gather | solution.py:17
  23.7 8.3 %fusion.81 = f32[2,320]{1,0:T(2,128)S(1)} fusion(bf16[1,2,320,4,128]{4,3,2,1,0:T(4,128)(2,1)} %param.12, f32[2,320]{1,0:T(2,128)S(1)} %sub.193), kind=kLoop, calls=%fused_computation.150 | loop fusion | flops 1310080 | bytes 660480 | tf_op jit(solution)/shard_map/reduce_sum | solution.py:62
  32.2 26.7 %psum.84 = f32[2,32]{1,0:T(2,128)S(1)} all-reduce(f32[2,32]{1,0:T(2,128)S(1)} %reduce_sum.328), channel_id=1, replica_groups=mesh['segment'=8,'patch'=16] {'patch'}, use_global_device_ids=true, to_apply=%region_5.6 | all-reduce | flops 64 | bytes 512 | tf_op jit(solution)/shard_map/psum | solution.py:62
  62.5 3.2 collective-permute-start.1
  65.7 3.2 collective-permute-start.4
  76.8 33.3 %psum.85 = f32[2,4,4,128]{3,1,2,0:T(4,128)S(1)} all-reduce(f32[2,4,4,128]{3,1,2,0:T(4,128)S(1)} %fusion.115), channel_id=1, replica_groups=mesh['segment'=8,'patch'=16] {'segment'}, use_global_device_ids=true, to_apply=%region_6.7 | all-reduce | flops 4096 | bytes 32768 | tf_op jit(solution)/shard_map/psum | solution.py:46
  110.2 9.9 %collective-permute-start.2 = (bf16[2,4,1,128]{3,1,2,0:T(4,128)(2,1)S(1)}, bf16[2,4,1,128]{3,1,2,0:T(4,128)(2,1)S(1)}, u32[]{:S(2)}, u32[]{:S(2)}) collective-permute-start(bf16[2,4,1,128]{3,1,2,0:T(4,128)(2,1)S(1)} %get-tuple-element.40), channel_id=1, source_target_pairs={{0,1},{1,2},{2,3},{3,4},{4,5},{5,6},{6,7},{7,8},{8,9},{9,10},{10,1... | collective-permute-start | bytes 6152 | tf_op jit(solution)/shard_map/ppermute | solution.py:30
  129.4 16.2 %all-gather.11 = f32[16,2,32]{2,1,0:T(2,128)S(1)} all-gather(f32[1,2,32]{2,1,0:T(2,128)S(1)} %bitcast.587), channel_id=3, replica_groups=mesh['segment'=8,'patch'=16] {'patch'}, dimensions={0}, use_global_device_ids=true | all-gather | bytes 4352 | tf_op jit(solution)/shard_map/all_gather | solution.py:17
  146.4 27.2 %psum.86 = f32[2,32]{1,0:T(2,128)S(1)} all-reduce(f32[2,32]{1,0:T(2,128)S(1)} %reduce_sum.341), channel_id=1, replica_groups=mesh['segment'=8,'patch'=16] {'patch'}, use_global_device_ids=true, to_apply=%region_12.13 | all-reduce | flops 64 | bytes 512 | tf_op jit(solution)/shard_map/psum | solution.py:62
  180.4 2.6 collective-permute-done.6
  196.4 16.2 %all-gather.12 = f32[16,2,32]{2,1,0:T(2,128)S(1)} all-gather(f32[1,2,32]{2,1,0:T(2,128)S(1)} %bitcast.588), channel_id=4, replica_groups=mesh['segment'=8,'patch'=16] {'patch'}, dimensions={0}, use_global_device_ids=true | all-gather | bytes 4352 | tf_op jit(solution)/shard_map/all_gather | solution.py:17
  213.4 26.7 %psum.87 = f32[2,32]{1,0:T(2,128)S(1)} all-reduce(f32[2,32]{1,0:T(2,128)S(1)} %reduce_sum.354), channel_id=1, replica_groups=mesh['segment'=8,'patch'=16] {'patch'}, use_global_device_ids=true, to_apply=%region_18.19 | all-reduce | flops 64 | bytes 512 | tf_op jit(solution)/shard_map/psum | solution.py:62
  263.1 16.2 %all-gather.13 = f32[16,2,32]{2,1,0:T(2,128)S(1)} all-gather(f32[1,2,32]{2,1,0:T(2,128)S(1)} %bitcast.589), channel_id=5, replica_groups=mesh['segment'=8,'patch'=16] {'patch'}, dimensions={0}, use_global_device_ids=true | all-gather | bytes 4352 | tf_op jit(solution)/shard_map/all_gather | solution.py:17
  280.1 26.7 %psum.88 = f32[2,32]{1,0:T(2,128)S(1)} all-reduce(f32[2,32]{1,0:T(2,128)S(1)} %reduce_sum.364), channel_id=1, replica_groups=mesh['segment'=8,'patch'=16] {'patch'}, use_global_device_ids=true, to_apply=%region_24.25 | all-reduce | flops 64 | bytes 512 | tf_op jit(solution)/shard_map/psum | solution.py:62
  313.7 2.6 collective-permute-done.10
  329.7 16.2 %all-gather.14 = f32[16,2,32]{2,1,0:T(2,128)S(1)} all-gather(f32[1,2,32]{2,1,0:T(2,128)S(1)} %bitcast.590), channel_id=6, replica_groups=mesh['segment'=8,'patch'=16] {'patch'}, dimensions={0}, use_global_device_ids=true | all-gather | bytes 4352 | tf_op jit(solution)/shard_map/all_gather | solution.py:17
  346.7 26.9 %psum.89 = f32[2,32]{1,0:T(2,128)S(1)} all-reduce(f32[2,32]{1,0:T(2,128)S(1)} %reduce_sum.444), channel_id=1, replica_groups=mesh['segment'=8,'patch'=16] {'patch'}, use_global_device_ids=true, to_apply=%region_30.31 | all-reduce | flops 64 | bytes 512 | tf_op jit(solution)/shard_map/psum | solution.py:62
  380.4 2.6 collective-permute-done.12
  396.7 16.2 %all-gather.15 = f32[16,2,32]{2,1,0:T(2,128)S(1)} all-gather(f32[1,2,32]{2,1,0:T(2,128)S(1)} %bitcast.591), channel_id=7, replica_groups=mesh['segment'=8,'patch'=16] {'patch'}, dimensions={0}, use_global_device_ids=true | all-gather | bytes 4352 | tf_op jit(solution)/shard_map/all_gather | solution.py:17
  415.7 27.3 %psum.90 = f32[2,32]{1,0:T(2,128)S(1)} all-reduce(f32[2,32]{1,0:T(2,128)S(1)} %reduce_sum.451), channel_id=1, replica_groups=mesh['segment'=8,'patch'=16] {'patch'}, use_global_device_ids=true, to_apply=%region_36.37 | all-reduce | flops 64 | bytes 512 | tf_op jit(solution)/shard_map/psum | solution.py:62
  449.7 2.6 collective-permute-done.14
  455.5 34.4 %psum.91 = f32[2,4,4,128]{3,1,2,0:T(4,128)S(1)} all-reduce(f32[2,4,4,128]{3,1,2,0:T(4,128)S(1)} %fusion.107), channel_id=1, replica_groups=mesh['segment'=8,'patch'=16] {'segment'}, use_global_device_ids=true, to_apply=%region_37.38 | all-reduce | flops 4096 | bytes 32768 | tf_op jit(solution)/shard_map/psum | solution.py:46
  490.0 9.5 %collective-permute-start.15 = (bf16[2,4,1,128]{3,1,2,0:T(4,128)(2,1)S(1)}, bf16[2,4,1,128]{3,1,2,0:T(4,128)(2,1)S(1)}, u32[]{:S(2)}, u32[]{:S(2)}) collective-permute-start(bf16[2,4,1,128]{3,1,2,0:T(4,128)(2,1)S(1)} %get-tuple-element.38), channel_id=1, source_target_pairs={{0,1},{1,2},{2,3},{3,4},{4,5},{5,6},{6,7},{7,8},{8,9},{9,10},{10,1... | collective-permute-start | bytes 6152 | tf_op jit(solution)/shard_map/ppermute | solution.py:30
  508.0 16.4 %all-gather.16 = f32[16,2,32]{2,1,0:T(2,128)S(1)} all-gather(f32[1,2,32]{2,1,0:T(2,128)S(1)} %bitcast.592), channel_id=8, replica_groups=mesh['segment'=8,'patch'=16] {'patch'}, dimensions={0}, use_global_device_ids=true | all-gather | bytes 4352 | tf_op jit(solution)/shard_map/all_gather | solution.py:17
  525.1 26.7 %psum.92 = f32[2,32]{1,0:T(2,128)S(1)} all-reduce(f32[2,32]{1,0:T(2,128)S(1)} %reduce_sum.458), channel_id=1, replica_groups=mesh['segment'=8,'patch'=16] {'patch'}, use_global_device_ids=true, to_apply=%region_43.44 | all-reduce | flops 64 | bytes 512 | tf_op jit(solution)/shard_map/psum | solution.py:62
  558.6 2.6 collective-permute-done.19
  574.7 16.2 %all-gather.17 = f32[16,2,32]{2,1,0:T(2,128)S(1)} all-gather(f32[1,2,32]{2,1,0:T(2,128)S(1)} %bitcast.593), channel_id=9, replica_groups=mesh['segment'=8,'patch'=16] {'patch'}, dimensions={0}, use_global_device_ids=true | all-gather | bytes 4352 | tf_op jit(solution)/shard_map/all_gather | solution.py:17
  591.7 26.7 %psum.93 = f32[2,32]{1,0:T(2,128)S(1)} all-reduce(f32[2,32]{1,0:T(2,128)S(1)} %reduce_sum.465), channel_id=1, replica_groups=mesh['segment'=8,'patch'=16] {'patch'}, use_global_device_ids=true, to_apply=%region_49.50 | all-reduce | flops 64 | bytes 512 | tf_op jit(solution)/shard_map/psum | solution.py:62
  641.3 16.2 %all-gather.18 = f32[16,2,32]{2,1,0:T(2,128)S(1)} all-gather(f32[1,2,32]{2,1,0:T(2,128)S(1)} %bitcast.594), channel_id=10, replica_groups=mesh['segment'=8,'patch'=16] {'patch'}, dimensions={0}, use_global_device_ids=true | all-gather | bytes 4352 | tf_op jit(solution)/shard_map/all_gather | solution.py:17
  658.3 26.7 %psum.94 = f32[2,32]{1,0:T(2,128)S(1)} all-reduce(f32[2,32]{1,0:T(2,128)S(1)} %reduce_sum.472), channel_id=1, replica_groups=mesh['segment'=8,'patch'=16] {'patch'}, use_global_device_ids=true, to_apply=%region_55.56 | all-reduce | flops 64 | bytes 512 | tf_op jit(solution)/shard_map/psum | solution.py:62
  707.9 16.2 %all-gather.19 = f32[16,2,32]{2,1,0:T(2,128)S(1)} all-gather(f32[1,2,32]{2,1,0:T(2,128)S(1)} %bitcast.595), channel_id=11, replica_groups=mesh['segment'=8,'patch'=16] {'patch'}, dimensions={0}, use_global_device_ids=true | all-gather | bytes 4352 | tf_op jit(solution)/shard_map/all_gather | solution.py:17
  724.8 26.9 %psum.95 = f32[2,32]{1,0:T(2,128)S(1)} all-reduce(f32[2,32]{1,0:T(2,128)S(1)} %reduce_sum.479), channel_id=1, replica_groups=mesh['segment'=8,'patch'=16] {'patch'}, use_global_device_ids=true, to_apply=%region_61.62 | all-reduce | flops 64 | bytes 512 | tf_op jit(solution)/shard_map/psum | solution.py:62
  (332 shorter events, 222.8 us)
Async XLA Ops:
  0.6 58.5 %copy-start = (bf16[1,2,320,4,128]{4,3,2,1,0:T(4,128)(2,1)S(1)}, bf16[1,2,320,4,128]{4,3,2,1,0:T(4,128)(2,1)}, u32[]{:S(2)}) copy-start(bf16[1,2,320,4,128]{4,3,2,1,0:T(4,128)(2,1)} %param.12) | copy-start | bytes 1966084
  0.6 58.5 %copy-start.4 = (f32[320]{0:T(512)S(1)}, f32[320]{0:T(512)}, u32[]{:S(2)}) copy-start(f32[320]{0:T(512)} %param.22) | copy-start | bytes 3844
  0.7 58.5 %copy-start.3 = (f32[320]{0:T(512)S(1)}, f32[320]{0:T(512)}, u32[]{:S(2)}) copy-start(f32[320]{0:T(512)} %param.23) | copy-start | bytes 3844
  60.5 11.3 %collective-permute-start = (bf16[2,320,1,128]{3,1,2,0:T(8,128)(2,1)}, bf16[2,320,1,128]{3,1,2,0:T(8,128)(2,1)}, u32[]{:S(2)}, u32[]{:S(2)}) collective-permute-start(bf16[2,320,1,128]{3,1,2,0:T(8,128)(2,1)} %get-tuple-element.36), channel_id=1, source_target_pairs={{0,1},{1,2},{2,3},{3,4},{4,5},{5,6},{6,7},{7,8},{8,9},{9,10},{10,1... | collective-permute-start | bytes 491528 | tf_op jit(solution)/shard_map/ppermute | solution.py:30
  62.5 9.3 %collective-permute-start.1 = (bf16[2,320,1,128]{3,1,2,0:T(8,128)(2,1)}, bf16[2,320,1,128]{3,1,2,0:T(8,128)(2,1)S(1)}, u32[]{:S(2)}, u32[]{:S(2)}) collective-permute-start(bf16[2,320,1,128]{3,1,2,0:T(8,128)(2,1)} %get-tuple-element.37), channel_id=1, source_target_pairs={{1,0},{2,1},{3,2},{4,3},{5,4},{6,5},{7,6},{8,7},{9,8},{10,9},{11,1... | collective-permute-start | bytes 491528 | tf_op jit(solution)/shard_map/ppermute | solution.py:33
  65.7 62.8 %collective-permute-start.4 = (bf16[2,320,4,128]{3,1,2,0:T(8,128)(2,1)S(1)}, bf16[2,320,4,128]{3,1,2,0:T(8,128)(2,1)S(1)}, u32[]{:S(2)}, u32[]{:S(2)}) collective-permute-start(bf16[2,320,4,128]{3,1,2,0:T(8,128)(2,1)S(1)} %bitcast.585), channel_id=1, source_target_pairs={{0,16},{16,32},{32,48},{48,64},{64,80},{80,96},{96,112},{1,17},{17... | collective-permute-start | bytes 1966088 | tf_op jit(solution)/shard_map/ppermute | solution.py:41
  76.2 44.0 %copy-start.5 = (f32[1,2,2,320]{3,2,1,0:T(2,128)S(1)}, f32[1,2,2,320]{3,2,1,0:T(2,128)}, u32[]{:S(2)}) copy-start(f32[1,2,2,320]{3,2,1,0:T(2,128)} %param.19) | copy-start | bytes 15364
  76.2 44.0 %copy-start.6 = (f32[1,2,2,320]{3,2,1,0:T(2,128)S(1)}, f32[1,2,2,320]{3,2,1,0:T(2,128)}, u32[]{:S(2)}) copy-start(f32[1,2,2,320]{3,2,1,0:T(2,128)} %param.18) | copy-start | bytes 15364
  76.2 46.6 %copy-start.1 = (bf16[9,320,4]{1,2,0:T(4,128)(2,1)S(1)}, bf16[9,320,4]{1,2,0:T(4,128)(2,1)}, u32[]{:S(2)}) copy-start(bf16[9,320,4]{1,2,0:T(4,128)(2,1)} %param.20) | copy-start | bytes 69124
  110.2 12.6 %collective-permute-start.2 = (bf16[2,4,1,128]{3,1,2,0:T(4,128)(2,1)S(1)}, bf16[2,4,1,128]{3,1,2,0:T(4,128)(2,1)S(1)}, u32[]{:S(2)}, u32[]{:S(2)}) collective-permute-start(bf16[2,4,1,128]{3,1,2,0:T(4,128)(2,1)S(1)} %get-tuple-element.40), channel_id=1, source_target_pairs={{0,1},{1,2},{2,3},{3,4},{4,5},{5,6},{6,7},{7,8},{8,9},{9,10},{10,1... | collective-permute-start | bytes 6152 | tf_op jit(solution)/shard_map/ppermute | solution.py:30
  120.9 4.9 collective-permute-start.3
  174.4 5.9 collective-permute-start.5
  176.4 6.6 collective-permute-start.6
  241.0 6.0 collective-permute-start.7
  242.9 6.6 collective-permute-start.8
  307.7 5.9 collective-permute-start.9
  309.7 6.6 collective-permute-start.10
  374.5 5.9 collective-permute-start.11
  376.4 6.6 collective-permute-start.12
  413.2 94.0 %collective-permute-start.17 = (bf16[2,320,4,128]{3,1,2,0:T(8,128)(2,1)S(1)}, bf16[2,320,4,128]{3,1,2,0:T(8,128)(2,1)S(1)}, u32[]{:S(2)}, u32[]{:S(2)}) collective-permute-start(bf16[2,320,4,128]{3,1,2,0:T(8,128)(2,1)S(1)} %get-tuple-element.55), channel_id=1, source_target_pairs={{0,16},{16,32},{32,48},{48,64},{64,80},{80,96},{96,112},{1,17},{17... | collective-permute-start | bytes 1966088 | tf_op jit(solution)/shard_map/ppermute | solution.py:41
  443.8 5.9 collective-permute-start.13
  445.7 6.6 collective-permute-start.14
  490.0 12.5 %collective-permute-start.15 = (bf16[2,4,1,128]{3,1,2,0:T(4,128)(2,1)S(1)}, bf16[2,4,1,128]{3,1,2,0:T(4,128)(2,1)S(1)}, u32[]{:S(2)}, u32[]{:S(2)}) collective-permute-start(bf16[2,4,1,128]{3,1,2,0:T(4,128)(2,1)S(1)} %get-tuple-element.38), channel_id=1, source_target_pairs={{0,1},{1,2},{2,3},{3,4},{4,5},{5,6},{6,7},{7,8},{8,9},{9,10},{10,1... | collective-permute-start | bytes 6152 | tf_op jit(solution)/shard_map/ppermute | solution.py:30
  499.5 4.9 collective-permute-start.16
  552.7 5.9 collective-permute-start.18
  554.6 6.6 collective-permute-start.19
  619.2 6.0 collective-permute-start.20
  621.1 6.6 collective-permute-start.21
  685.9 5.9 collective-permute-start.22
  687.8 6.6 collective-permute-start.23
  752.6 5.9 collective-permute-start.24
  754.5 6.6 collective-permute-start.25
  (3 other events, 49.1 us)
